TPU v7x, 128 devices: a whole 4x4x4 slice. The times are simulated.
128 devices in a mesh: grp: 8 (over z, core), dir: 16 (over x, y).
Axes of the slice: x: 4, y: 4, z: 4, core: 2. Of those that a mesh axis runs over, the one named last changes fastest.
Arguments:
- incident: float32 [4, 1024, 256, 128], P(None, ('grp', 'dir')), may hold values from -6 to 6
- currents_past: bfloat16 [2, 1024, 256, 128], P(None, ('grp', 'dir')), may hold values from -6 to 6
- spectra_past: bfloat16 [2, 128, 1152, 128], P(None, ('grp', 'dir')), may hold values from -9 to 9
- self_inverse: bfloat16 [1024, 256, 256], P(('grp', 'dir')), may hold values from -0.25 to 0.25
- near_blocks: bfloat16 [1024, 6, 2, 256, 256], P(('grp', 'dir')), may hold values from -0.078125 to 0.078125
- neighbours: int32 [1024, 6], P(('grp', 'dir')), may hold values from 0 to 1023, as said below
- near_mask: int32 [1024, 6], P(('grp', 'dir')), may hold values 0 or 1
- ray_out: bfloat16 [256, 1152], replicated, may hold values from -0.375 to 0.375
- ray_in: bfloat16 [1152, 256], replicated, may hold values from -0.1875 to 0.1875
- child_shift: float32 [8, 1152], replicated, may hold values from -1 to 1
- far_sources: int32 [128, 16], replicated, may hold values from 0 to 127
- far_delays: int32 [128, 16], replicated, may hold values from 1 to 2
- translation: float32 [128, 16, 1152], P(None, None, ('grp', 'dir')), may hold values from -0.75 to 0.75
Outputs:
- currents: bfloat16 [4, 1024, 256, 128], P(None, ('grp', 'dir'))
Inputs may be any that keep to these rules, and one draw needn't show every extreme that they name: `neighbours`: the entry of group g names a group held by the same device as g, by the device just before it or by the one just after it, devices counted in the order grp then dir, each holding 8 consecutive groups.
All inputs are finite; a program needn't handle non-finite values. No bound on the sum of `near_mask` on one device may be relied on, other than what follows from the above.
Results may differ from a plain program's by a relative error of at most 0.0095.
Values may be sent and summed in bfloat16 or wider, within the bound.
No kernel may reach another device: no remote copies, remote signals or barrier semaphores. Data moves between devices by JAX's collectives and lax.ppermute only.
A program may use at most 128 MiB of HBM per device.

v0:
```python
import functools

import jax
import jax.numpy as jnp
import numpy as np
from jax import lax
from jax.experimental import pallas as pl
from jax.experimental.pallas import tpu as pltpu
from jax.sharding import PartitionSpec as P

LAGS = 2
STEPS = 4
AXES = ("grp", "dir")
CHUNK = 16
UNIT = 2
BF16 = jnp.bfloat16
F32 = jnp.float32
HBM = pl.BlockSpec(memory_space=pltpu.HBM)


def params():
    return pltpu.CompilerParams(vmem_limit_bytes=64 << 20)


def matmul(left, right):
    return jnp.dot(left, right, preferred_element_type=F32)


def spread_matrix(band, rows):
    out = np.zeros((CHUNK * rows, CHUNK * band), np.float32)
    for b in range(CHUNK):
        for i in range(band):
            out[b * rows + i, b * band + i] = 1.0
    return out


def lagged_spread(band, rows):
    out = np.zeros((LAGS, CHUNK * LAGS * rows, CHUNK * band), np.float32)
    for lag in range(LAGS):
        for b in range(CHUNK):
            for i in range(band):
                out[lag, (b * LAGS + lag) * rows + i, b * band + i] = 1.0
    return out


def pack_kernel(select_ref, past_ref, out_ref):
    tall, wide = select_ref.shape[1], select_ref.shape[2]
    for m in range(past_ref.shape[1] // wide):
        total = matmul(select_ref[0], past_ref[0, pl.ds(m * wide, wide), :])
        for lag in range(1, LAGS):
            total += matmul(select_ref[lag], past_ref[lag, pl.ds(m * wide, wide), :])
        out_ref[pl.ds(m * tall, tall), :] = total.astype(BF16)


def pack(past, band, rows):
    select = jnp.asarray(lagged_spread(band, rows), BF16)
    messages = past.shape[1] // band
    return pl.pallas_call(
        pack_kernel,
        out_shape=jax.ShapeDtypeStruct((messages * LAGS * rows, past.shape[2]), BF16),
        compiler_params=params(),
        name="pack",
    )(select, past)


def rays_kernel(select_ref, ray_in_ref, ray_out_ref, shift_ref, in_ref, out_ref, shift_out_ref):
    tall, wide = select_ref.shape
    select = select_ref[...]
    outgoing = ray_out_ref[...].astype(F32).T
    shift = shift_ref[...]
    shift = jnp.concatenate([shift, jnp.zeros((128 - shift.shape[0], shift.shape[1]), F32)]).T
    incoming = []
    for m in range(ray_in_ref.shape[0] // wide):
        at, to = m * wide, pl.ds(m * tall, tall)
        incoming.append(matmul(select, ray_in_ref[pl.ds(at, wide), :]))
        out_ref[to, :] = matmul(select, outgoing[at : at + wide, :].astype(BF16)).astype(BF16)
        shift_out_ref[to, :] = matmul(select, shift[at : at + wide, :].astype(BF16)).astype(BF16)
    in_ref[...] = jnp.concatenate(incoming).T.astype(BF16)


def pad_rays(ray_in, ray_out, child_shift, band, rows):
    select = jnp.asarray(spread_matrix(band, rows), BF16)
    padded = ray_in.shape[0] // band * rows
    return pl.pallas_call(
        rays_kernel,
        out_shape=(
            jax.ShapeDtypeStruct((ray_in.shape[1], padded), BF16),
            jax.ShapeDtypeStruct((padded, ray_out.shape[0]), BF16),
            jax.ShapeDtypeStruct((padded, 128), BF16),
        ),
        compiler_params=params(),
        name="rays",
    )(select, ray_in, ray_out, child_shift)


def weights_kernel(sources_ref, delays_ref, table_ref, out_ref):
    band, entries, parents = table_ref.shape
    slots = LAGS * parents
    slot = lax.broadcasted_iota(jnp.int32, (slots, parents), 0)
    wanted = (delays_ref[...] - 1) * parents + sources_ref[...]
    for k in range(band):
        total = jnp.zeros((slots, parents), F32)
        for f in range(entries):
            total += jnp.where(slot == wanted[f : f + 1, :], table_ref[k, f : f + 1, :], 0.0)
        out_ref[k] = total.T.astype(BF16)


def far_weights(far_sources, far_delays, translation):
    parents, _, band = translation.shape
    return pl.pallas_call(
        weights_kernel,
        out_shape=jax.ShapeDtypeStruct((band, parents, LAGS * parents), BF16),
        compiler_params=params(),
        name="weights",
    )(far_sources.T, far_delays.T, jnp.transpose(translation, (2, 1, 0)))


def translate_kernel(rows, places, weights_ref, *refs):
    inputs, out_ref, wide, result_ref = refs[:-4], refs[-4], refs[-3:-1], refs[-1]
    band, parents, _ = weights_ref.shape
    for source, scratch in zip(inputs, wide):
        scratch[: source.shape[0], :] = source[...].astype(F32)
    result_ref[...] = jnp.zeros_like(result_ref)
    for k in range(band):
        picked = [
            wide[array][pl.ds(start + k, parents, stride=stride), :].astype(BF16)
            for array, start, stride in places
        ]
        total = matmul(weights_ref[k], jnp.concatenate(picked, axis=0))
        result_ref[pl.ds(k, parents, stride=rows), :] = total
    out_ref[...] = result_ref[...].astype(BF16)


def translate(weights, rows, newest, oldest):
    _, parents, _ = weights.shape
    arrays, places = [], []
    for array, start, stride in (newest, oldest):
        known = [i for i, other in enumerate(arrays) if other is array]
        if not known:
            arrays.append(array)
        places.append((known[0] if known else len(arrays) - 1, start, stride))
    columns = newest[0].shape[1]
    longest = max(array.shape[0] for array in arrays)
    return pl.pallas_call(
        functools.partial(translate_kernel, rows, tuple(places)),
        out_shape=jax.ShapeDtypeStruct((parents * rows, columns), BF16),
        scratch_shapes=[
            pltpu.VMEM((longest, columns), F32),
            pltpu.VMEM((longest, columns), F32),
            pltpu.VMEM((parents * rows, columns), F32),
        ],
        compiler_params=params(),
        name="translate",
    )(weights, *arrays)


def near_kernel(step, leads, first_ref, ids_ref, mask_ref, incident_ref, blocks_ref, *refs):
    sources, refs = refs[: 3 * LAGS], refs[3 * LAGS :]
    out_ref, window_ref, matrices_ref, field_ref, sems, block_sems, out_sems = refs
    groups, slots = matrices_ref.shape[:2]
    parts = groups // UNIT
    dead = window_ref.shape[1] - 1

    def load(i):
        chosen = pl.ds(i * UNIT, UNIT)
        return pltpu.make_async_copy(blocks_ref.at[chosen], matrices_ref.at[chosen], block_sems.at[i])

    def save(i):
        chosen = pl.ds(i * UNIT, UNIT)
        return pltpu.make_async_copy(field_ref.at[chosen], out_ref.at[chosen], out_sems.at[i])

    moves = [pltpu.make_async_copy(incident_ref.at[step], field_ref, sems.at[0])]
    for index, lead in enumerate(leads):
        for side in range(3):
            source = sources[index * 3 + side]
            target = window_ref.at[index, pl.ds(side * groups, groups)]
            moves.append(
                pltpu.make_async_copy(
                    source if lead is None else source.at[lead], target, sems.at[index * 3 + side + 1]
                )
            )
    for move in moves:
        move.start()
    for i in range(2):
        load(i).start()
    for index in range(LAGS):
        window_ref[index, dead] = jnp.zeros(window_ref.shape[2:], window_ref.dtype)
    for move in moves:
        move.wait()

    def body(i, carry):
        load(i).wait()

        @pl.when(i + 2 < parts)
        def _():
            load(i + 2).start()

        for j in range(UNIT):
            g = i * UNIT + j
            total = field_ref[g]
            for n in range(slots):
                picked = jnp.where(mask_ref[g, n] != 0, ids_ref[g, n] - first_ref[0], dead)
                for index in range(LAGS):
                    total -= matmul(matrices_ref[g, n, index], window_ref[index, picked])
            field_ref[g] = total
        save(i).start()
        return carry

    lax.fori_loop(0, parts, body, 0)
    for i in range(parts):
        save(i).wait()


def near_field(places, incident, step, near_blocks, windows):
    groups, slots, _, unknowns, _ = near_blocks.shape
    columns = incident.shape[-1]
    arrays = [array for parts, _ in windows for array in parts]
    leads = tuple(lead for _, lead in windows)
    return pl.pallas_call(
        functools.partial(near_kernel, step, leads),
        in_specs=[pl.BlockSpec(memory_space=pltpu.SMEM)] * 3 + [HBM] * (2 + len(arrays)),
        out_specs=HBM,
        out_shape=jax.ShapeDtypeStruct((groups, unknowns, columns), F32),
        scratch_shapes=[
            pltpu.VMEM((LAGS, 3 * groups + 1, unknowns, columns), BF16),
            pltpu.VMEM((groups, slots, LAGS, unknowns, unknowns), BF16),
            pltpu.VMEM((groups, unknowns, columns), F32),
            pltpu.SemaphoreType.DMA((3 * LAGS + 1,)),
            pltpu.SemaphoreType.DMA((groups // UNIT,)),
            pltpu.SemaphoreType.DMA((groups // UNIT,)),
        ],
        compiler_params=params(),
        name="near",
    )(*places, incident, near_blocks, *arrays)


def solve_kernel(step, aliased, *refs):
    last = step == STEPS - 1
    inputs = refs[:6]
    count = 1 if last else 3
    outs = refs[6 + aliased : 6 + aliased + count]
    scratch = refs[6 + aliased + count :]
    buffers, (currents_ref, spectra_ref, in_sems, out_sems) = scratch[:6], scratch[6:]
    loads = [
        pltpu.make_async_copy(source, buffer, in_sems.at[i])
        for i, (source, buffer) in enumerate(zip(inputs, buffers))
        if not (last and i == 5)
    ]
    for load in loads:
        load.start()
    arriving_ref, in_ref, shift_ref, base_ref, inverse_ref, outward_ref = buffers
    children, _, columns = base_ref.shape
    pairs = [(c, c + 1) for c in range(0, children, 2)]
    stores = []

    def store(source, target):
        stores.append(pltpu.make_async_copy(source, target, out_sems.at[len(stores)]))
        stores[-1].start()

    for i in range(3):
        loads[i].wait()
    arriving = arriving_ref[...]
    fields = []
    for pair in pairs:
        received = jnp.concatenate(
            [shift_ref[:, d : d + 1] * arriving for d in pair], axis=1
        )
        fields.append(matmul(in_ref[...], received))
    for i in range(3, 5):
        loads[i].wait()
    for pair, field in zip(pairs, fields):
        for i, d in enumerate(pair):
            drive = (base_ref[d] - field[:, i * columns : (i + 1) * columns]).astype(BF16)
            currents_ref[d] = matmul(inverse_ref[d], drive).astype(BF16)
    store(currents_ref, outs[0].at[step])
    if not last:
        store(currents_ref, outs[1])
        loads[5].wait()
        spectra = None
        for pair in pairs:
            spread = matmul(
                outward_ref[...], jnp.concatenate([currents_ref[d] for d in pair], axis=1)
            )
            for i, d in enumerate(pair):
                term = shift_ref[:, d : d + 1].astype(F32) * spread[:, i * columns : (i + 1) * columns]
                spectra = term if spectra is None else spectra + term
        spectra_ref[...] = spectra.astype(BF16)
        store(spectra_ref, outs[2])
    for copy in stores:
        copy.wait()


def solve(step, results, arriving, base, self_inverse, ray_in, ray_out, shift):
    last = step == STEPS - 1
    groups, unknowns, columns = base.shape
    operands = [arriving, ray_in, shift, base, self_inverse, ray_out]
    buffers = [pltpu.VMEM(a.shape, a.dtype) for a in operands]
    aliased = results is not None
    out_shape = [jax.ShapeDtypeStruct((STEPS, groups, unknowns, columns), BF16)]
    if not last:
        out_shape += [
            jax.ShapeDtypeStruct((groups, unknowns, columns), BF16),
            jax.ShapeDtypeStruct(arriving.shape, BF16),
        ]
    if aliased:
        operands.append(results)
    return pl.pallas_call(
        functools.partial(solve_kernel, step, aliased),
        in_specs=[HBM] * len(operands),
        out_specs=[HBM] * len(out_shape),
        out_shape=out_shape,
        input_output_aliases={len(operands) - 1: 0} if aliased else {},
        scratch_shapes=buffers
        + [
            pltpu.VMEM((groups, unknowns, columns), BF16),
            pltpu.VMEM(arriving.shape, BF16),
            pltpu.SemaphoreType.DMA((6,)),
            pltpu.SemaphoreType.DMA((3,)),
        ],
        compiler_params=params(),
        name="solve",
    )(*operands)


def shifted(block, distance):
    devices = range(lax.axis_size(AXES))
    route = [(i - distance, i) for i in devices if i - distance in devices]
    return lax.ppermute(block, AXES, route)


def window(block):
    return [shifted(block, 1), block, shifted(block, -1)]


def exchange(block, messages):
    tall, columns = block.shape
    cut = block.reshape(messages, tall // messages // 2, 2, columns)
    moved = lax.all_to_all(cut, AXES, split_axis=0, concat_axis=0, tiled=True)
    return moved.reshape(tall, columns)


def on_device(
    incident,
    currents_past,
    spectra_past,
    self_inverse,
    near_blocks,
    neighbours,
    near_mask,
    ray_out,
    ray_in,
    child_shift,
    far_sources,
    far_delays,
    translation,
):
    groups = self_inverse.shape[0]
    messages, band = translation.shape[0], translation.shape[2]
    rows = band + band % 2
    first_group = (lax.axis_index(AXES) - 1) * groups
    places = (first_group.reshape(1), neighbours, near_mask)
    packed = pack(spectra_past[:, 0], band, rows)
    opening = exchange(packed, messages)
    past = window(currents_past)
    bands = [(opening, lag * rows, LAGS * rows) for lag in range(LAGS)]
    windows = [(past, 0), (past, 1)]
    rays = pad_rays(ray_in, ray_out, child_shift, band, rows)
    weights = far_weights(far_sources, far_delays, translation)
    weights, rays = lax.optimization_barrier((weights, rays))
    results = None
    for step in range(STEPS):
        arriving = exchange(translate(weights, rows, *bands), messages)
        base = near_field(places, incident, step, near_blocks, windows)
        results, *rest = solve(step, results, arriving, base, self_inverse, *rays)
        if rest:
            current, spectra = rest
            moved = exchange(spectra, messages)
            nearby = window(current)
            windows = [(nearby, None), windows[0]]
            bands = [(moved, 0, rows), bands[0]]
    return results


def solution(mesh):
    in_specs = (
        P(None, AXES, None, None),
        P(None, AXES, None, None),
        P(None, AXES, None, None),
        P(AXES, None, None),
        P(AXES, None, None, None, None),
        P(AXES, None),
        P(AXES, None),
        P(),
        P(),
        P(),
        P(),
        P(),
        P(None, None, AXES),
    )
    out_specs = P(None, AXES, None, None)
    return jax.shard_map(
        on_device, mesh=mesh, in_specs=in_specs, out_specs=out_specs, check_vma=False
    )
```

profile of v0, /device:TPU:1, one launch (start us, length us, event | category | flops | bytes accessed | tf_op | source)
XLA Modules:
  0.0 218.5 jit_solution(278075948797586982)
XLA Ops:
  0.0 8.2 %collective-permute-start.1 = (bf16[2,8,256,128]{3,2,1,0:T(8,128)(2,1)}, bf16[2,8,256,128]{3,2,1,0:T(8,128)(2,1)}, u32[]{:S(2)}, u32[]{:S(2)}) collective-permute-start(bf16[2,8,256,128]{3,2,1,0:T(8,128)(2,1)} %refs_4_.8), channel_id=1, source_target_pairs={{1,0},{2,1},{3,2},{4,3},{5,4},{6,5},{7,6},{8,7},{9,8},{10,9},{11,1... | collective-permute-start | bytes 3145736 | tf_op jit(solution)/shard_map/ppermute | solution.py:328
  13.0 10.4 %all-to-all-start = ((bf16[128,10,2,128]{3,2,1,0:T(2,128)(2,1)}), bf16[128,10,2,128]{3,2,1,0:T(2,128)(2,1)}, u32[]{:S(2)}, u32[]{:S(2)}) async-start(bf16[128,10,2,128]{3,2,1,0:T(2,128)(2,1)} %bitcast.21), calls=%async_computation | async-start | bytes 1310720 | tf_op jit(solution)/shard_map/all_to_all | solution.py:338
  30.4 22.4 %all-to-all-done = bf16[128,10,2,128]{3,2,1,0:T(2,128)(2,1)} async-done(((bf16[128,10,2,128]{3,2,1,0:T(2,128)(2,1)}), bf16[128,10,2,128]{3,2,1,0:T(2,128)(2,1)}, u32[]{:S(2)}, u32[]{:S(2)}) %all-to-all-start) | async-done | bytes 655392 | tf_op jit(solution)/shard_map/all_to_all | solution.py:338
  55.2 4.6 %all-to-all-start.1 = ((bf16[128,5,2,128]{3,2,1,0:T(2,128)(2,1)}), bf16[128,5,2,128]{3,2,1,0:T(2,128)(2,1)}, u32[]{:S(2)}, u32[]{:S(2)}) async-start(bf16[128,5,2,128]{3,2,1,0:T(2,128)(2,1)} %bitcast.22), calls=%async_computation.1 | async-start | bytes 655360 | tf_op jit(solution)/shard_map/all_to_all | solution.py:338
  59.8 9.0 %near.4.refs_3_ = f32[8,256,128]{2,1,0:T(8,128)} custom-call(s32[1]{0:T(128)} %bitcast.8.first_ref, s32[8,6]{1,0:T(8,128)} %ids_ref.7, s32[8,6]{1,0:T(8,128)} %mask_ref.7, f32[4,8,256,128]{3,2,1,0:T(8,128)} %incident_ref.7, bf16[8,6,2,256,256]{4,3,2,1,0:T(8,128)(2,1)} %blocks_ref.7, bf16[2,8,256,128]{3,2,1,0:T(8,128)(2,1)} %collective-permute-done.refs_0_.refs_3_, ...), custom_call_target="tpu_custom_call" | custom-call | tf_op jit(solution)/shard_map/near/pallas_call | solution.py:219
  70.4 5.1 %solve.4 = (bf16[4,8,256,128]{3,2,1,0:T(8,128)(2,1)}, bf16[8,256,128]{2,1,0:T(8,128)(2,1)}, bf16[1280,128]{1,0:T(8,128)(2,1)}) custom-call(bf16[1280,128]{1,0:T(8,128)(2,1)} %bitcast.7.refs_0_, bf16[256,1280]{1,0:T(8,128)(2,1)} %get-tuple-element.25.refs_1_, bf16[1280,128]{1,0:T(8,128)(2,1)} %get-tuple-element.26.refs_2_, f32[8,256,128]{2,1,0:T(8,128)} %near.4.refs_3_, ...), custom_call_target="tpu_custom_call" | custom-call | tf_op jit(solution)/shard_map/solve/pallas_call | solution.py:307
  75.5 8.0 %all-to-all-start.2 = ((bf16[128,5,2,128]{3,2,1,0:T(2,128)(2,1)}), bf16[128,5,2,128]{3,2,1,0:T(2,128)(2,1)}, u32[]{:S(2)}, u32[]{:S(2)}) async-start(bf16[128,5,2,128]{3,2,1,0:T(2,128)(2,1)} %bitcast.29), calls=%async_computation.2 | async-start | bytes 655360 | tf_op jit(solution)/shard_map/all_to_all | solution.py:338
  83.5 7.0 %collective-permute-start.3 = (bf16[8,256,128]{2,1,0:T(8,128)(2,1)}, bf16[8,256,128]{2,1,0:T(8,128)(2,1)}, u32[]{:S(2)}, u32[]{:S(2)}) collective-permute-start(bf16[8,256,128]{2,1,0:T(8,128)(2,1)} %get-tuple-element.29.refs_1_.refs_4_), channel_id=1, source_target_pairs={{1,0},{2,1},{3,2},{4,3},{5,4},{6,5},{7,6},{8,7},{9,8},{10,9},{11,1... | collective-permute-start | bytes 1572872 | tf_op jit(solution)/shard_map/ppermute | solution.py:328
  97.3 8.1 %all-to-all-start.3 = ((bf16[128,5,2,128]{3,2,1,0:T(2,128)(2,1)}), bf16[128,5,2,128]{3,2,1,0:T(2,128)(2,1)}, u32[]{:S(2)}, u32[]{:S(2)}) async-start(bf16[128,5,2,128]{3,2,1,0:T(2,128)(2,1)} %bitcast.25), calls=%async_computation.3 | async-start | bytes 655360 | tf_op jit(solution)/shard_map/all_to_all | solution.py:338
  105.4 5.3 %collective-permute-done.2.refs_0_.refs_3_ = bf16[8,256,128]{2,1,0:T(8,128)(2,1)} collective-permute-done((bf16[8,256,128]{2,1,0:T(8,128)(2,1)}, bf16[8,256,128]{2,1,0:T(8,128)(2,1)}, u32[]{:S(2)}, u32[]{:S(2)}) %collective-permute-start.2) | collective-permute-done | bytes 524320 | tf_op jit(solution)/shard_map/ppermute | solution.py:328
  110.7 8.9 %near.5.refs_3_ = f32[8,256,128]{2,1,0:T(8,128)} custom-call(s32[1]{0:T(128)} %bitcast.8.first_ref, s32[8,6]{1,0:T(8,128)} %ids_ref.7, s32[8,6]{1,0:T(8,128)} %mask_ref.7, f32[4,8,256,128]{3,2,1,0:T(8,128)} %incident_ref.7, bf16[8,6,2,256,256]{4,3,2,1,0:T(8,128)(2,1)} %blocks_ref.7, bf16[8,256,128]{2,1,0:T(8,128)(2,1)} %collective-permute-done.2.refs_0_.refs_3_, ...), custom_call_target="tpu_custom_call" | custom-call | tf_op jit(solution)/shard_map/near/pallas_call | solution.py:219
  119.7 5.1 %solve.5 = (bf16[4,8,256,128]{3,2,1,0:T(8,128)(2,1)}, bf16[8,256,128]{2,1,0:T(8,128)(2,1)}, bf16[1280,128]{1,0:T(8,128)(2,1)}) custom-call(bf16[1280,128]{1,0:T(8,128)(2,1)} %bitcast.12.refs_0_, bf16[256,1280]{1,0:T(8,128)(2,1)} %get-tuple-element.25.refs_1_, bf16[1280,128]{1,0:T(8,128)(2,1)} %get-tuple-element.26.refs_2_, ...), custom_call_target="tpu_custom_call", output_to_operand_aliasing={{0}: (6, {})} | custom-call | tf_op jit(solution)/shard_map/solve/pallas_call | solution.py:307
  124.8 5.9 %all-to-all-start.4 = ((bf16[128,5,2,128]{3,2,1,0:T(2,128)(2,1)}), bf16[128,5,2,128]{3,2,1,0:T(2,128)(2,1)}, u32[]{:S(2)}, u32[]{:S(2)}) async-start(bf16[128,5,2,128]{3,2,1,0:T(2,128)(2,1)} %bitcast.27), calls=%async_computation.4 | async-start | bytes 655360 | tf_op jit(solution)/shard_map/all_to_all | solution.py:338
  130.7 7.0 %collective-permute-start.5 = (bf16[8,256,128]{2,1,0:T(8,128)(2,1)}, bf16[8,256,128]{2,1,0:T(8,128)(2,1)}, u32[]{:S(2)}, u32[]{:S(2)}) collective-permute-start(bf16[8,256,128]{2,1,0:T(8,128)(2,1)} %get-tuple-element.32.refs_1_.refs_4_), channel_id=1, source_target_pairs={{1,0},{2,1},{3,2},{4,3},{5,4},{6,5},{7,6},{8,7},{9,8},{10,9},{11,1... | collective-permute-start | bytes 1572872 | tf_op jit(solution)/shard_map/ppermute | solution.py:328
  144.2 8.1 %all-to-all-start.5 = ((bf16[128,5,2,128]{3,2,1,0:T(2,128)(2,1)}), bf16[128,5,2,128]{3,2,1,0:T(2,128)(2,1)}, u32[]{:S(2)}, u32[]{:S(2)}) async-start(bf16[128,5,2,128]{3,2,1,0:T(2,128)(2,1)} %bitcast.24), calls=%async_computation.5 | async-start | bytes 655360 | tf_op jit(solution)/shard_map/all_to_all | solution.py:338
  152.3 5.6 %collective-permute-done.4.refs_0_.refs_3_ = bf16[8,256,128]{2,1,0:T(8,128)(2,1)} collective-permute-done((bf16[8,256,128]{2,1,0:T(8,128)(2,1)}, bf16[8,256,128]{2,1,0:T(8,128)(2,1)}, u32[]{:S(2)}, u32[]{:S(2)}) %collective-permute-start.4) | collective-permute-done | bytes 524320 | tf_op jit(solution)/shard_map/ppermute | solution.py:328
  157.9 9.0 %near.6.refs_3_ = f32[8,256,128]{2,1,0:T(8,128)} custom-call(s32[1]{0:T(128)} %bitcast.8.first_ref, s32[8,6]{1,0:T(8,128)} %ids_ref.7, s32[8,6]{1,0:T(8,128)} %mask_ref.7, f32[4,8,256,128]{3,2,1,0:T(8,128)} %incident_ref.7, bf16[8,6,2,256,256]{4,3,2,1,0:T(8,128)(2,1)} %blocks_ref.7, bf16[8,256,128]{2,1,0:T(8,128)(2,1)} %collective-permute-done.4.refs_0_.refs_3_, ...), custom_call_target="tpu_custom_call" | custom-call | tf_op jit(solution)/shard_map/near/pallas_call | solution.py:219
  166.8 5.1 %solve.6 = (bf16[4,8,256,128]{3,2,1,0:T(8,128)(2,1)}, bf16[8,256,128]{2,1,0:T(8,128)(2,1)}, bf16[1280,128]{1,0:T(8,128)(2,1)}) custom-call(bf16[1280,128]{1,0:T(8,128)(2,1)} %bitcast.16.refs_0_, bf16[256,1280]{1,0:T(8,128)(2,1)} %get-tuple-element.25.refs_1_, bf16[1280,128]{1,0:T(8,128)(2,1)} %get-tuple-element.26.refs_2_, ...), custom_call_target="tpu_custom_call", output_to_operand_aliasing={{0}: (6, {})} | custom-call | tf_op jit(solution)/shard_map/solve/pallas_call | solution.py:307
  172.0 5.9 %all-to-all-start.6 = ((bf16[128,5,2,128]{3,2,1,0:T(2,128)(2,1)}), bf16[128,5,2,128]{3,2,1,0:T(2,128)(2,1)}, u32[]{:S(2)}, u32[]{:S(2)}) async-start(bf16[128,5,2,128]{3,2,1,0:T(2,128)(2,1)} %bitcast.28), calls=%async_computation.6 | async-start | bytes 655360 | tf_op jit(solution)/shard_map/all_to_all | solution.py:338
  177.9 7.0 %collective-permute-start.7 = (bf16[8,256,128]{2,1,0:T(8,128)(2,1)}, bf16[8,256,128]{2,1,0:T(8,128)(2,1)}, u32[]{:S(2)}, u32[]{:S(2)}) collective-permute-start(bf16[8,256,128]{2,1,0:T(8,128)(2,1)} %get-tuple-element.35.refs_1_), channel_id=1, source_target_pairs={{1,0},{2,1},{3,2},{4,3},{5,4},{6,5},{7,6},{8,7},{9,8},{10,9},{11,1... | collective-permute-start | bytes 1572872 | tf_op jit(solution)/shard_map/ppermute | solution.py:328
  191.4 8.1 %all-to-all-start.7 = ((bf16[128,5,2,128]{3,2,1,0:T(2,128)(2,1)}), bf16[128,5,2,128]{3,2,1,0:T(2,128)(2,1)}, u32[]{:S(2)}, u32[]{:S(2)}) async-start(bf16[128,5,2,128]{3,2,1,0:T(2,128)(2,1)} %bitcast.23), calls=%async_computation.7 | async-start | bytes 655360 | tf_op jit(solution)/shard_map/all_to_all | solution.py:338
  199.5 5.5 %collective-permute-done.6.refs_0_ = bf16[8,256,128]{2,1,0:T(8,128)(2,1)} collective-permute-done((bf16[8,256,128]{2,1,0:T(8,128)(2,1)}, bf16[8,256,128]{2,1,0:T(8,128)(2,1)}, u32[]{:S(2)}, u32[]{:S(2)}) %collective-permute-start.6) | collective-permute-done | bytes 524320 | tf_op jit(solution)/shard_map/ppermute | solution.py:328
  205.0 9.0 %near.7.refs_3_ = f32[8,256,128]{2,1,0:T(8,128)} custom-call(s32[1]{0:T(128)} %bitcast.8.first_ref, s32[8,6]{1,0:T(8,128)} %ids_ref.7, s32[8,6]{1,0:T(8,128)} %mask_ref.7, f32[4,8,256,128]{3,2,1,0:T(8,128)} %incident_ref.7, bf16[8,6,2,256,256]{4,3,2,1,0:T(8,128)(2,1)} %blocks_ref.7, bf16[8,256,128]{2,1,0:T(8,128)(2,1)} %collective-permute-done.6.refs_0_, ...), custom_call_target="tpu_custom_call" | custom-call | tf_op jit(solution)/shard_map/near/pallas_call | solution.py:219
  214.0 4.3 %solve.7 = bf16[4,8,256,128]{3,2,1,0:T(8,128)(2,1)} custom-call(bf16[1280,128]{1,0:T(8,128)(2,1)} %bitcast.20.refs_0_, bf16[256,1280]{1,0:T(8,128)(2,1)} %get-tuple-element.25.refs_1_, bf16[1280,128]{1,0:T(8,128)(2,1)} %get-tuple-element.26.refs_2_, f32[8,256,128]{2,1,0:T(8,128)} %near.7.refs_3_, ...), custom_call_target="tpu_custom_call", output_to_operand_aliasing={{}: (6, {})} | custom-call | tf_op jit(solution)/shard_map/solve/pallas_call | solution.py:307
  (23 shorter events, 35.6 us)
Async XLA Ops:
  0.0 59.8 %collective-permute-start.1 = (bf16[2,8,256,128]{3,2,1,0:T(8,128)(2,1)}, bf16[2,8,256,128]{3,2,1,0:T(8,128)(2,1)}, u32[]{:S(2)}, u32[]{:S(2)}) collective-permute-start(bf16[2,8,256,128]{3,2,1,0:T(8,128)(2,1)} %refs_4_.8), channel_id=1, source_target_pairs={{1,0},{2,1},{3,2},{4,3},{5,4},{6,5},{7,6},{8,7},{9,8},{10,9},{11,1... | collective-permute-start | bytes 3145736 | tf_op jit(solution)/shard_map/ppermute | solution.py:328
  8.2 51.6 %collective-permute-start = (bf16[2,8,256,128]{3,2,1,0:T(8,128)(2,1)}, bf16[2,8,256,128]{3,2,1,0:T(8,128)(2,1)}, u32[]{:S(2)}, u32[]{:S(2)}) collective-permute-start(bf16[2,8,256,128]{3,2,1,0:T(8,128)(2,1)} %refs_4_.8), channel_id=1, source_target_pairs={{0,1},{1,2},{2,3},{3,4},{4,5},{5,6},{6,7},{7,8},{8,9},{9,10},{10,1... | collective-permute-start | bytes 3145736 | tf_op jit(solution)/shard_map/ppermute | solution.py:328
  13.0 39.8 %all-to-all-start = ((bf16[128,10,2,128]{3,2,1,0:T(2,128)(2,1)}), bf16[128,10,2,128]{3,2,1,0:T(2,128)(2,1)}, u32[]{:S(2)}, u32[]{:S(2)}) async-start(bf16[128,10,2,128]{3,2,1,0:T(2,128)(2,1)} %bitcast.21), calls=%async_computation | async-start | bytes 1310720 | tf_op jit(solution)/shard_map/all_to_all | solution.py:338
  55.2 15.2 %all-to-all-start.1 = ((bf16[128,5,2,128]{3,2,1,0:T(2,128)(2,1)}), bf16[128,5,2,128]{3,2,1,0:T(2,128)(2,1)}, u32[]{:S(2)}, u32[]{:S(2)}) async-start(bf16[128,5,2,128]{3,2,1,0:T(2,128)(2,1)} %bitcast.22), calls=%async_computation.1 | async-start | bytes 655360 | tf_op jit(solution)/shard_map/all_to_all | solution.py:338
  75.5 19.2 %all-to-all-start.2 = ((bf16[128,5,2,128]{3,2,1,0:T(2,128)(2,1)}), bf16[128,5,2,128]{3,2,1,0:T(2,128)(2,1)}, u32[]{:S(2)}, u32[]{:S(2)}) async-start(bf16[128,5,2,128]{3,2,1,0:T(2,128)(2,1)} %bitcast.29), calls=%async_computation.2 | async-start | bytes 655360 | tf_op jit(solution)/shard_map/all_to_all | solution.py:338
  83.5 21.8 %collective-permute-start.3 = (bf16[8,256,128]{2,1,0:T(8,128)(2,1)}, bf16[8,256,128]{2,1,0:T(8,128)(2,1)}, u32[]{:S(2)}, u32[]{:S(2)}) collective-permute-start(bf16[8,256,128]{2,1,0:T(8,128)(2,1)} %get-tuple-element.29.refs_1_.refs_4_), channel_id=1, source_target_pairs={{1,0},{2,1},{3,2},{4,3},{5,4},{6,5},{7,6},{8,7},{9,8},{10,9},{11,1... | collective-permute-start | bytes 1572872 | tf_op jit(solution)/shard_map/ppermute | solution.py:328
  90.5 20.2 %collective-permute-start.2 = (bf16[8,256,128]{2,1,0:T(8,128)(2,1)}, bf16[8,256,128]{2,1,0:T(8,128)(2,1)}, u32[]{:S(2)}, u32[]{:S(2)}) collective-permute-start(bf16[8,256,128]{2,1,0:T(8,128)(2,1)} %get-tuple-element.29.refs_1_.refs_4_), channel_id=1, source_target_pairs={{0,1},{1,2},{2,3},{3,4},{4,5},{5,6},{6,7},{7,8},{8,9},{9,10},{10,1... | collective-permute-start | bytes 1572872 | tf_op jit(solution)/shard_map/ppermute | solution.py:328
  97.3 22.4 %all-to-all-start.3 = ((bf16[128,5,2,128]{3,2,1,0:T(2,128)(2,1)}), bf16[128,5,2,128]{3,2,1,0:T(2,128)(2,1)}, u32[]{:S(2)}, u32[]{:S(2)}) async-start(bf16[128,5,2,128]{3,2,1,0:T(2,128)(2,1)} %bitcast.25), calls=%async_computation.3 | async-start | bytes 655360 | tf_op jit(solution)/shard_map/all_to_all | solution.py:338
  124.8 17.0 %all-to-all-start.4 = ((bf16[128,5,2,128]{3,2,1,0:T(2,128)(2,1)}), bf16[128,5,2,128]{3,2,1,0:T(2,128)(2,1)}, u32[]{:S(2)}, u32[]{:S(2)}) async-start(bf16[128,5,2,128]{3,2,1,0:T(2,128)(2,1)} %bitcast.27), calls=%async_computation.4 | async-start | bytes 655360 | tf_op jit(solution)/shard_map/all_to_all | solution.py:338
  130.7 21.6 %collective-permute-start.5 = (bf16[8,256,128]{2,1,0:T(8,128)(2,1)}, bf16[8,256,128]{2,1,0:T(8,128)(2,1)}, u32[]{:S(2)}, u32[]{:S(2)}) collective-permute-start(bf16[8,256,128]{2,1,0:T(8,128)(2,1)} %get-tuple-element.32.refs_1_.refs_4_), channel_id=1, source_target_pairs={{1,0},{2,1},{3,2},{4,3},{5,4},{6,5},{7,6},{8,7},{9,8},{10,9},{11,1... | collective-permute-start | bytes 1572872 | tf_op jit(solution)/shard_map/ppermute | solution.py:328
  137.6 20.2 %collective-permute-start.4 = (bf16[8,256,128]{2,1,0:T(8,128)(2,1)}, bf16[8,256,128]{2,1,0:T(8,128)(2,1)}, u32[]{:S(2)}, u32[]{:S(2)}) collective-permute-start(bf16[8,256,128]{2,1,0:T(8,128)(2,1)} %get-tuple-element.32.refs_1_.refs_4_), channel_id=1, source_target_pairs={{0,1},{1,2},{2,3},{3,4},{4,5},{5,6},{6,7},{7,8},{8,9},{9,10},{10,1... | collective-permute-start | bytes 1572872 | tf_op jit(solution)/shard_map/ppermute | solution.py:328
  144.2 22.6 %all-to-all-start.5 = ((bf16[128,5,2,128]{3,2,1,0:T(2,128)(2,1)}), bf16[128,5,2,128]{3,2,1,0:T(2,128)(2,1)}, u32[]{:S(2)}, u32[]{:S(2)}) async-start(bf16[128,5,2,128]{3,2,1,0:T(2,128)(2,1)} %bitcast.24), calls=%async_computation.5 | async-start | bytes 655360 | tf_op jit(solution)/shard_map/all_to_all | solution.py:338
  172.0 17.0 %all-to-all-start.6 = ((bf16[128,5,2,128]{3,2,1,0:T(2,128)(2,1)}), bf16[128,5,2,128]{3,2,1,0:T(2,128)(2,1)}, u32[]{:S(2)}, u32[]{:S(2)}) async-start(bf16[128,5,2,128]{3,2,1,0:T(2,128)(2,1)} %bitcast.28), calls=%async_computation.6 | async-start | bytes 655360 | tf_op jit(solution)/shard_map/all_to_all | solution.py:338
  177.9 21.6 %collective-permute-start.7 = (bf16[8,256,128]{2,1,0:T(8,128)(2,1)}, bf16[8,256,128]{2,1,0:T(8,128)(2,1)}, u32[]{:S(2)}, u32[]{:S(2)}) collective-permute-start(bf16[8,256,128]{2,1,0:T(8,128)(2,1)} %get-tuple-element.35.refs_1_), channel_id=1, source_target_pairs={{1,0},{2,1},{3,2},{4,3},{5,4},{6,5},{7,6},{8,7},{9,8},{10,9},{11,1... | collective-permute-start | bytes 1572872 | tf_op jit(solution)/shard_map/ppermute | solution.py:328
  184.8 20.2 %collective-permute-start.6 = (bf16[8,256,128]{2,1,0:T(8,128)(2,1)}, bf16[8,256,128]{2,1,0:T(8,128)(2,1)}, u32[]{:S(2)}, u32[]{:S(2)}) collective-permute-start(bf16[8,256,128]{2,1,0:T(8,128)(2,1)} %get-tuple-element.35.refs_1_), channel_id=1, source_target_pairs={{0,1},{1,2},{2,3},{3,4},{4,5},{5,6},{6,7},{7,8},{8,9},{9,10},{10,1... | collective-permute-start | bytes 1572872 | tf_op jit(solution)/shard_map/ppermute | solution.py:328
  191.4 22.6 %all-to-all-start.7 = ((bf16[128,5,2,128]{3,2,1,0:T(2,128)(2,1)}), bf16[128,5,2,128]{3,2,1,0:T(2,128)(2,1)}, u32[]{:S(2)}, u32[]{:S(2)}) async-start(bf16[128,5,2,128]{3,2,1,0:T(2,128)(2,1)} %bitcast.23), calls=%async_computation.7 | async-start | bytes 655360 | tf_op jit(solution)/shard_map/all_to_all | solution.py:338
where the time goes:
time: 220 us; the launch traced here: 219 us
  starting transfers between devices  95.9 us (44%)
  Pallas kernels  75.2 us (34%)
  waiting for transfers between devices  47.1 us (21%)
    all_to_all x8, starting transfers between devices, exchange(): moved = lax.all_to_all(cut, AXES, split_axis=0, concat_axis=0, tiled=True)  59.1 us
    ppermute x8, starting transfers between devices, shifted(): return lax.ppermute(block, AXES, route)  36.8 us
    pallas_call x4, Pallas kernels, near_field(): pl.pallas_call(functools.partial(near_kernel, step, leads), in_specs=[pl....  35.8 us
    all_to_all x8, waiting for transfers between devices, exchange(): moved = lax.all_to_all(cut, AXES, split_axis=0, concat_axis=0, tiled=True)  30.6 us
    pallas_call x4, Pallas kernels, solve(): pl.pallas_call(functools.partial(solve_kernel, step, aliased), in_specs=[...  19.7 us
    ppermute x8, waiting for transfers between devices, shifted(): return lax.ppermute(block, AXES, route)  16.4 us
    pallas_call x4, Pallas kernels, translate(): pl.pallas_call(functools.partial(translate_kernel, rows, tuple(places)),...  9.84 us
  transfers between devices with their start and end apart: 16, of which 8 were waited for; matrix products, arithmetic and copies ran while one was open for 0% of the time, Pallas kernels for 25%

commit v1 on v0

--- a/solution.py
+++ b/solution.py
@@ -12,7 +12,8 @@
 STEPS = 4
 AXES = ("grp", "dir")
 CHUNK = 16
-UNIT = 2
+UNIT = 1
+PIECES = 4
 BF16 = jnp.bfloat16
 F32 = jnp.float32
 HBM = pl.BlockSpec(memory_space=pltpu.HBM)
@@ -34,33 +35,54 @@
     return out
 
 
-def lagged_spread(band, rows):
-    out = np.zeros((LAGS, CHUNK * LAGS * rows, CHUNK * band), np.float32)
-    for lag in range(LAGS):
-        for b in range(CHUNK):
-            for i in range(band):
-                out[lag, (b * LAGS + lag) * rows + i, b * band + i] = 1.0
-    return out
-
-
-def pack_kernel(select_ref, past_ref, out_ref):
-    tall, wide = select_ref.shape[1], select_ref.shape[2]
-    for m in range(past_ref.shape[1] // wide):
-        total = matmul(select_ref[0], past_ref[0, pl.ds(m * wide, wide), :])
-        for lag in range(1, LAGS):
-            total += matmul(select_ref[lag], past_ref[lag, pl.ds(m * wide, wide), :])
-        out_ref[pl.ds(m * tall, tall), :] = total.astype(BF16)
+def pack_kernel(rows, past_ref, out_ref, taken_ref, wide_ref, result_ref, rounded_ref, in_sems, out_sems):
+    lags, directions, columns = past_ref.shape
+    parents = out_ref.shape[0] // (lags * rows)
+    band = directions // parents
+    part = out_ref.shape[0] // PIECES
+    loads = [
+        pltpu.make_async_copy(past_ref.at[lag], taken_ref.at[lag], in_sems.at[lag]) for lag in range(lags)
+    ]
+    for load in loads:
+        load.start()
+    for lag in range(lags):
+        for k in range(band, rows):
+            result_ref[pl.ds(lag * rows + k, parents, stride=lags * rows), :] = jnp.zeros((parents, columns), F32)
+        loads[lag].wait()
+        wide_ref[lag] = taken_ref[lag].astype(F32)
+        for k in range(band):
+            result_ref[pl.ds(lag * rows + k, parents, stride=lags * rows), :] = wide_ref[
+                lag, pl.ds(k, parents, stride=band), :
+            ]
+    stores = []
+    for piece in range(PIECES):
+        chosen = pl.ds(piece * part, part)
+        rounded_ref[chosen, :] = result_ref[chosen, :].astype(BF16)
+        stores.append(pltpu.make_async_copy(rounded_ref.at[chosen], out_ref.at[chosen], out_sems.at[piece]))
+        stores[-1].start()
+    for store in stores:
+        store.wait()
 
 
 def pack(past, band, rows):
-    select = jnp.asarray(lagged_spread(band, rows), BF16)
-    messages = past.shape[1] // band
-    return pl.pallas_call(
-        pack_kernel,
-        out_shape=jax.ShapeDtypeStruct((messages * LAGS * rows, past.shape[2]), BF16),
+    lags, directions, columns = past.shape
+    tall = directions // band * lags * rows
+    return pl.pallas_call(
+        functools.partial(pack_kernel, rows),
+        in_specs=[HBM],
+        out_specs=HBM,
+        out_shape=jax.ShapeDtypeStruct((tall, columns), BF16),
+        scratch_shapes=[
+            pltpu.VMEM(past.shape, BF16),
+            pltpu.VMEM(past.shape, F32),
+            pltpu.VMEM((tall, columns), F32),
+            pltpu.VMEM((tall, columns), BF16),
+            pltpu.SemaphoreType.DMA((lags,)),
+            pltpu.SemaphoreType.DMA((PIECES,)),
+        ],
         compiler_params=params(),
         name="pack",
-    )(select, past)
+    )(past)
 
 
 def rays_kernel(select_ref, ray_in_ref, ray_out_ref, shift_ref, in_ref, out_ref, shift_out_ref):
@@ -181,7 +203,7 @@
             )
     for move in moves:
         move.start()
-    for i in range(2):
+    for i in range(3):
         load(i).start()
     for index in range(LAGS):
         window_ref[index, dead] = jnp.zeros(window_ref.shape[2:], window_ref.dtype)
@@ -191,9 +213,9 @@
     def body(i, carry):
         load(i).wait()
 
-        @pl.when(i + 2 < parts)
+        @pl.when(i + 3 < parts)
         def _():
-            load(i + 2).start()
+            load(i + 3).start()
 
         for j in range(UNIT):
             g = i * UNIT + j

time: 220 us -> 219 us (level)
  no operation moved by 1% of the time
where the time goes in v1:
time: 219 us; the launch traced here: 218 us
  starting transfers between devices  95.7 us (44%)
  Pallas kernels  73.7 us (34%)
  waiting for transfers between devices  48 us (22%)
    all_to_all x8, starting transfers between devices, exchange(): moved = lax.all_to_all(cut, AXES, split_axis=0, concat_axis=0, tiled=True)  58.9 us
    ppermute x8, starting transfers between devices, shifted(): return lax.ppermute(block, AXES, route)  36.8 us
    pallas_call x4, Pallas kernels, near_field(): pl.pallas_call(functools.partial(near_kernel, step, leads), in_specs=[pl....  35.1 us
    all_to_all x8, waiting for transfers between devices, exchange(): moved = lax.all_to_all(cut, AXES, split_axis=0, concat_axis=0, tiled=True)  31.6 us
    pallas_call x4, Pallas kernels, solve(): pl.pallas_call(functools.partial(solve_kernel, step, aliased), in_specs=[...  19.7 us
    ppermute x8, waiting for transfers between devices, shifted(): return lax.ppermute(block, AXES, route)  16.4 us
    pallas_call x4, Pallas kernels, translate(): pl.pallas_call(functools.partial(translate_kernel, rows, tuple(places)),...  9.84 us
  transfers between devices with their start and end apart: 16, of which 8 were waited for; matrix products, arithmetic and copies ran while one was open for 0% of the time, Pallas kernels for 25%

profile of v1, /device:TPU:1, one launch (start us, length us, event | category | flops | bytes accessed | tf_op | source)
XLA Modules:
  0.0 217.8 jit_solution(585282380673360873)
XLA Ops:
  0.0 8.2 %collective-permute-start.1 = (bf16[2,8,256,128]{3,2,1,0:T(8,128)(2,1)}, bf16[2,8,256,128]{3,2,1,0:T(8,128)(2,1)}, u32[]{:S(2)}, u32[]{:S(2)}) collective-permute-start(bf16[2,8,256,128]{3,2,1,0:T(8,128)(2,1)} %refs_4_.8), channel_id=1, source_target_pairs={{1,0},{2,1},{3,2},{4,3},{5,4},{6,5},{7,6},{8,7},{9,8},{10,9},{11,1... | collective-permute-start | bytes 3145736 | tf_op jit(solution)/shard_map/ppermute | solution.py:350
  12.2 10.4 %all-to-all-start = ((bf16[128,10,2,128]{3,2,1,0:T(2,128)(2,1)}), bf16[128,10,2,128]{3,2,1,0:T(2,128)(2,1)}, u32[]{:S(2)}, u32[]{:S(2)}) async-start(bf16[128,10,2,128]{3,2,1,0:T(2,128)(2,1)} %bitcast.21), calls=%async_computation | async-start | bytes 1310720 | tf_op jit(solution)/shard_map/all_to_all | solution.py:360
  29.6 23.2 %all-to-all-done = bf16[128,10,2,128]{3,2,1,0:T(2,128)(2,1)} async-done(((bf16[128,10,2,128]{3,2,1,0:T(2,128)(2,1)}), bf16[128,10,2,128]{3,2,1,0:T(2,128)(2,1)}, u32[]{:S(2)}, u32[]{:S(2)}) %all-to-all-start) | async-done | bytes 655392 | tf_op jit(solution)/shard_map/all_to_all | solution.py:360
  55.2 4.6 %all-to-all-start.1 = ((bf16[128,5,2,128]{3,2,1,0:T(2,128)(2,1)}), bf16[128,5,2,128]{3,2,1,0:T(2,128)(2,1)}, u32[]{:S(2)}, u32[]{:S(2)}) async-start(bf16[128,5,2,128]{3,2,1,0:T(2,128)(2,1)} %bitcast.22), calls=%async_computation.1 | async-start | bytes 655360 | tf_op jit(solution)/shard_map/all_to_all | solution.py:360
  59.8 8.8 %near.4.refs_3_ = f32[8,256,128]{2,1,0:T(8,128)} custom-call(s32[1]{0:T(128)} %bitcast.8.first_ref, s32[8,6]{1,0:T(8,128)} %ids_ref.7, s32[8,6]{1,0:T(8,128)} %mask_ref.7, f32[4,8,256,128]{3,2,1,0:T(8,128)} %incident_ref.7, bf16[8,6,2,256,256]{4,3,2,1,0:T(8,128)(2,1)} %blocks_ref.7, bf16[2,8,256,128]{3,2,1,0:T(8,128)(2,1)} %collective-permute-done.refs_0_.refs_3_, ...), custom_call_target="tpu_custom_call" | custom-call | tf_op jit(solution)/shard_map/near/pallas_call | solution.py:241
  70.4 5.1 %solve.4 = (bf16[4,8,256,128]{3,2,1,0:T(8,128)(2,1)}, bf16[8,256,128]{2,1,0:T(8,128)(2,1)}, bf16[1280,128]{1,0:T(8,128)(2,1)}) custom-call(bf16[1280,128]{1,0:T(8,128)(2,1)} %bitcast.7.refs_0_, bf16[256,1280]{1,0:T(8,128)(2,1)} %get-tuple-element.25.refs_1_, bf16[1280,128]{1,0:T(8,128)(2,1)} %get-tuple-element.26.refs_2_, f32[8,256,128]{2,1,0:T(8,128)} %near.4.refs_3_, ...), custom_call_target="tpu_custom_call" | custom-call | tf_op jit(solution)/shard_map/solve/pallas_call | solution.py:329
  75.5 7.9 %all-to-all-start.2 = ((bf16[128,5,2,128]{3,2,1,0:T(2,128)(2,1)}), bf16[128,5,2,128]{3,2,1,0:T(2,128)(2,1)}, u32[]{:S(2)}, u32[]{:S(2)}) async-start(bf16[128,5,2,128]{3,2,1,0:T(2,128)(2,1)} %bitcast.29), calls=%async_computation.2 | async-start | bytes 655360 | tf_op jit(solution)/shard_map/all_to_all | solution.py:360
  83.4 7.0 %collective-permute-start.3 = (bf16[8,256,128]{2,1,0:T(8,128)(2,1)}, bf16[8,256,128]{2,1,0:T(8,128)(2,1)}, u32[]{:S(2)}, u32[]{:S(2)}) collective-permute-start(bf16[8,256,128]{2,1,0:T(8,128)(2,1)} %get-tuple-element.29.refs_1_.refs_4_), channel_id=1, source_target_pairs={{1,0},{2,1},{3,2},{4,3},{5,4},{6,5},{7,6},{8,7},{9,8},{10,9},{11,1... | collective-permute-start | bytes 1572872 | tf_op jit(solution)/shard_map/ppermute | solution.py:350
  97.1 8.1 %all-to-all-start.3 = ((bf16[128,5,2,128]{3,2,1,0:T(2,128)(2,1)}), bf16[128,5,2,128]{3,2,1,0:T(2,128)(2,1)}, u32[]{:S(2)}, u32[]{:S(2)}) async-start(bf16[128,5,2,128]{3,2,1,0:T(2,128)(2,1)} %bitcast.25), calls=%async_computation.3 | async-start | bytes 655360 | tf_op jit(solution)/shard_map/all_to_all | solution.py:360
  105.2 5.3 %collective-permute-done.2.refs_0_.refs_3_ = bf16[8,256,128]{2,1,0:T(8,128)(2,1)} collective-permute-done((bf16[8,256,128]{2,1,0:T(8,128)(2,1)}, bf16[8,256,128]{2,1,0:T(8,128)(2,1)}, u32[]{:S(2)}, u32[]{:S(2)}) %collective-permute-start.2) | collective-permute-done | bytes 524320 | tf_op jit(solution)/shard_map/ppermute | solution.py:350
  110.5 8.8 %near.5.refs_3_ = f32[8,256,128]{2,1,0:T(8,128)} custom-call(s32[1]{0:T(128)} %bitcast.8.first_ref, s32[8,6]{1,0:T(8,128)} %ids_ref.7, s32[8,6]{1,0:T(8,128)} %mask_ref.7, f32[4,8,256,128]{3,2,1,0:T(8,128)} %incident_ref.7, bf16[8,6,2,256,256]{4,3,2,1,0:T(8,128)(2,1)} %blocks_ref.7, bf16[8,256,128]{2,1,0:T(8,128)(2,1)} %collective-permute-done.2.refs_0_.refs_3_, ...), custom_call_target="tpu_custom_call" | custom-call | tf_op jit(solution)/shard_map/near/pallas_call | solution.py:241
  119.3 5.1 %solve.5 = (bf16[4,8,256,128]{3,2,1,0:T(8,128)(2,1)}, bf16[8,256,128]{2,1,0:T(8,128)(2,1)}, bf16[1280,128]{1,0:T(8,128)(2,1)}) custom-call(bf16[1280,128]{1,0:T(8,128)(2,1)} %bitcast.12.refs_0_, bf16[256,1280]{1,0:T(8,128)(2,1)} %get-tuple-element.25.refs_1_, bf16[1280,128]{1,0:T(8,128)(2,1)} %get-tuple-element.26.refs_2_, ...), custom_call_target="tpu_custom_call", output_to_operand_aliasing={{0}: (6, {})} | custom-call | tf_op jit(solution)/shard_map/solve/pallas_call | solution.py:329
  124.4 5.9 %all-to-all-start.4 = ((bf16[128,5,2,128]{3,2,1,0:T(2,128)(2,1)}), bf16[128,5,2,128]{3,2,1,0:T(2,128)(2,1)}, u32[]{:S(2)}, u32[]{:S(2)}) async-start(bf16[128,5,2,128]{3,2,1,0:T(2,128)(2,1)} %bitcast.27), calls=%async_computation.4 | async-start | bytes 655360 | tf_op jit(solution)/shard_map/all_to_all | solution.py:360
  130.3 7.0 %collective-permute-start.5 = (bf16[8,256,128]{2,1,0:T(8,128)(2,1)}, bf16[8,256,128]{2,1,0:T(8,128)(2,1)}, u32[]{:S(2)}, u32[]{:S(2)}) collective-permute-start(bf16[8,256,128]{2,1,0:T(8,128)(2,1)} %get-tuple-element.32.refs_1_.refs_4_), channel_id=1, source_target_pairs={{1,0},{2,1},{3,2},{4,3},{5,4},{6,5},{7,6},{8,7},{9,8},{10,9},{11,1... | collective-permute-start | bytes 1572872 | tf_op jit(solution)/shard_map/ppermute | solution.py:350
  143.8 8.1 %all-to-all-start.5 = ((bf16[128,5,2,128]{3,2,1,0:T(2,128)(2,1)}), bf16[128,5,2,128]{3,2,1,0:T(2,128)(2,1)}, u32[]{:S(2)}, u32[]{:S(2)}) async-start(bf16[128,5,2,128]{3,2,1,0:T(2,128)(2,1)} %bitcast.24), calls=%async_computation.5 | async-start | bytes 655360 | tf_op jit(solution)/shard_map/all_to_all | solution.py:360
  151.9 5.6 %collective-permute-done.4.refs_0_.refs_3_ = bf16[8,256,128]{2,1,0:T(8,128)(2,1)} collective-permute-done((bf16[8,256,128]{2,1,0:T(8,128)(2,1)}, bf16[8,256,128]{2,1,0:T(8,128)(2,1)}, u32[]{:S(2)}, u32[]{:S(2)}) %collective-permute-start.4) | collective-permute-done | bytes 524320 | tf_op jit(solution)/shard_map/ppermute | solution.py:350
  157.5 8.8 %near.6.refs_3_ = f32[8,256,128]{2,1,0:T(8,128)} custom-call(s32[1]{0:T(128)} %bitcast.8.first_ref, s32[8,6]{1,0:T(8,128)} %ids_ref.7, s32[8,6]{1,0:T(8,128)} %mask_ref.7, f32[4,8,256,128]{3,2,1,0:T(8,128)} %incident_ref.7, bf16[8,6,2,256,256]{4,3,2,1,0:T(8,128)(2,1)} %blocks_ref.7, bf16[8,256,128]{2,1,0:T(8,128)(2,1)} %collective-permute-done.4.refs_0_.refs_3_, ...), custom_call_target="tpu_custom_call" | custom-call | tf_op jit(solution)/shard_map/near/pallas_call | solution.py:241
  166.3 5.1 %solve.6 = (bf16[4,8,256,128]{3,2,1,0:T(8,128)(2,1)}, bf16[8,256,128]{2,1,0:T(8,128)(2,1)}, bf16[1280,128]{1,0:T(8,128)(2,1)}) custom-call(bf16[1280,128]{1,0:T(8,128)(2,1)} %bitcast.16.refs_0_, bf16[256,1280]{1,0:T(8,128)(2,1)} %get-tuple-element.25.refs_1_, bf16[1280,128]{1,0:T(8,128)(2,1)} %get-tuple-element.26.refs_2_, ...), custom_call_target="tpu_custom_call", output_to_operand_aliasing={{0}: (6, {})} | custom-call | tf_op jit(solution)/shard_map/solve/pallas_call | solution.py:329
  171.4 5.9 %all-to-all-start.6 = ((bf16[128,5,2,128]{3,2,1,0:T(2,128)(2,1)}), bf16[128,5,2,128]{3,2,1,0:T(2,128)(2,1)}, u32[]{:S(2)}, u32[]{:S(2)}) async-start(bf16[128,5,2,128]{3,2,1,0:T(2,128)(2,1)} %bitcast.28), calls=%async_computation.6 | async-start | bytes 655360 | tf_op jit(solution)/shard_map/all_to_all | solution.py:360
  177.4 7.0 %collective-permute-start.7 = (bf16[8,256,128]{2,1,0:T(8,128)(2,1)}, bf16[8,256,128]{2,1,0:T(8,128)(2,1)}, u32[]{:S(2)}, u32[]{:S(2)}) collective-permute-start(bf16[8,256,128]{2,1,0:T(8,128)(2,1)} %get-tuple-element.35.refs_1_), channel_id=1, source_target_pairs={{1,0},{2,1},{3,2},{4,3},{5,4},{6,5},{7,6},{8,7},{9,8},{10,9},{11,1... | collective-permute-start | bytes 1572872 | tf_op jit(solution)/shard_map/ppermute | solution.py:350
  190.9 8.1 %all-to-all-start.7 = ((bf16[128,5,2,128]{3,2,1,0:T(2,128)(2,1)}), bf16[128,5,2,128]{3,2,1,0:T(2,128)(2,1)}, u32[]{:S(2)}, u32[]{:S(2)}) async-start(bf16[128,5,2,128]{3,2,1,0:T(2,128)(2,1)} %bitcast.23), calls=%async_computation.7 | async-start | bytes 655360 | tf_op jit(solution)/shard_map/all_to_all | solution.py:360
  199.0 5.5 %collective-permute-done.6.refs_0_ = bf16[8,256,128]{2,1,0:T(8,128)(2,1)} collective-permute-done((bf16[8,256,128]{2,1,0:T(8,128)(2,1)}, bf16[8,256,128]{2,1,0:T(8,128)(2,1)}, u32[]{:S(2)}, u32[]{:S(2)}) %collective-permute-start.6) | collective-permute-done | bytes 524320 | tf_op jit(solution)/shard_map/ppermute | solution.py:350
  204.5 8.8 %near.7.refs_3_ = f32[8,256,128]{2,1,0:T(8,128)} custom-call(s32[1]{0:T(128)} %bitcast.8.first_ref, s32[8,6]{1,0:T(8,128)} %ids_ref.7, s32[8,6]{1,0:T(8,128)} %mask_ref.7, f32[4,8,256,128]{3,2,1,0:T(8,128)} %incident_ref.7, bf16[8,6,2,256,256]{4,3,2,1,0:T(8,128)(2,1)} %blocks_ref.7, bf16[8,256,128]{2,1,0:T(8,128)(2,1)} %collective-permute-done.6.refs_0_, ...), custom_call_target="tpu_custom_call" | custom-call | tf_op jit(solution)/shard_map/near/pallas_call | solution.py:241
  213.3 4.3 %solve.7 = bf16[4,8,256,128]{3,2,1,0:T(8,128)(2,1)} custom-call(bf16[1280,128]{1,0:T(8,128)(2,1)} %bitcast.20.refs_0_, bf16[256,1280]{1,0:T(8,128)(2,1)} %get-tuple-element.25.refs_1_, bf16[1280,128]{1,0:T(8,128)(2,1)} %get-tuple-element.26.refs_2_, f32[8,256,128]{2,1,0:T(8,128)} %near.7.refs_3_, ...), custom_call_target="tpu_custom_call", output_to_operand_aliasing={{}: (6, {})} | custom-call | tf_op jit(solution)/shard_map/solve/pallas_call | solution.py:329
  (23 shorter events, 35.0 us)
Async XLA Ops:
  0.0 59.8 %collective-permute-start.1 = (bf16[2,8,256,128]{3,2,1,0:T(8,128)(2,1)}, bf16[2,8,256,128]{3,2,1,0:T(8,128)(2,1)}, u32[]{:S(2)}, u32[]{:S(2)}) collective-permute-start(bf16[2,8,256,128]{3,2,1,0:T(8,128)(2,1)} %refs_4_.8), channel_id=1, source_target_pairs={{1,0},{2,1},{3,2},{4,3},{5,4},{6,5},{7,6},{8,7},{9,8},{10,9},{11,1... | collective-permute-start | bytes 3145736 | tf_op jit(solution)/shard_map/ppermute | solution.py:350
  8.2 51.6 %collective-permute-start = (bf16[2,8,256,128]{3,2,1,0:T(8,128)(2,1)}, bf16[2,8,256,128]{3,2,1,0:T(8,128)(2,1)}, u32[]{:S(2)}, u32[]{:S(2)}) collective-permute-start(bf16[2,8,256,128]{3,2,1,0:T(8,128)(2,1)} %refs_4_.8), channel_id=1, source_target_pairs={{0,1},{1,2},{2,3},{3,4},{4,5},{5,6},{6,7},{7,8},{8,9},{9,10},{10,1... | collective-permute-start | bytes 3145736 | tf_op jit(solution)/shard_map/ppermute | solution.py:350
  12.2 40.5 %all-to-all-start = ((bf16[128,10,2,128]{3,2,1,0:T(2,128)(2,1)}), bf16[128,10,2,128]{3,2,1,0:T(2,128)(2,1)}, u32[]{:S(2)}, u32[]{:S(2)}) async-start(bf16[128,10,2,128]{3,2,1,0:T(2,128)(2,1)} %bitcast.21), calls=%async_computation | async-start | bytes 1310720 | tf_op jit(solution)/shard_map/all_to_all | solution.py:360
  55.2 15.2 %all-to-all-start.1 = ((bf16[128,5,2,128]{3,2,1,0:T(2,128)(2,1)}), bf16[128,5,2,128]{3,2,1,0:T(2,128)(2,1)}, u32[]{:S(2)}, u32[]{:S(2)}) async-start(bf16[128,5,2,128]{3,2,1,0:T(2,128)(2,1)} %bitcast.22), calls=%async_computation.1 | async-start | bytes 655360 | tf_op jit(solution)/shard_map/all_to_all | solution.py:360
  75.5 19.0 %all-to-all-start.2 = ((bf16[128,5,2,128]{3,2,1,0:T(2,128)(2,1)}), bf16[128,5,2,128]{3,2,1,0:T(2,128)(2,1)}, u32[]{:S(2)}, u32[]{:S(2)}) async-start(bf16[128,5,2,128]{3,2,1,0:T(2,128)(2,1)} %bitcast.29), calls=%async_computation.2 | async-start | bytes 655360 | tf_op jit(solution)/shard_map/all_to_all | solution.py:360
  83.4 21.8 %collective-permute-start.3 = (bf16[8,256,128]{2,1,0:T(8,128)(2,1)}, bf16[8,256,128]{2,1,0:T(8,128)(2,1)}, u32[]{:S(2)}, u32[]{:S(2)}) collective-permute-start(bf16[8,256,128]{2,1,0:T(8,128)(2,1)} %get-tuple-element.29.refs_1_.refs_4_), channel_id=1, source_target_pairs={{1,0},{2,1},{3,2},{4,3},{5,4},{6,5},{7,6},{8,7},{9,8},{10,9},{11,1... | collective-permute-start | bytes 1572872 | tf_op jit(solution)/shard_map/ppermute | solution.py:350
  90.4 20.2 %collective-permute-start.2 = (bf16[8,256,128]{2,1,0:T(8,128)(2,1)}, bf16[8,256,128]{2,1,0:T(8,128)(2,1)}, u32[]{:S(2)}, u32[]{:S(2)}) collective-permute-start(bf16[8,256,128]{2,1,0:T(8,128)(2,1)} %get-tuple-element.29.refs_1_.refs_4_), channel_id=1, source_target_pairs={{0,1},{1,2},{2,3},{3,4},{4,5},{5,6},{6,7},{7,8},{8,9},{9,10},{10,1... | collective-permute-start | bytes 1572872 | tf_op jit(solution)/shard_map/ppermute | solution.py:350
  97.1 22.2 %all-to-all-start.3 = ((bf16[128,5,2,128]{3,2,1,0:T(2,128)(2,1)}), bf16[128,5,2,128]{3,2,1,0:T(2,128)(2,1)}, u32[]{:S(2)}, u32[]{:S(2)}) async-start(bf16[128,5,2,128]{3,2,1,0:T(2,128)(2,1)} %bitcast.25), calls=%async_computation.3 | async-start | bytes 655360 | tf_op jit(solution)/shard_map/all_to_all | solution.py:360
  124.4 17.0 %all-to-all-start.4 = ((bf16[128,5,2,128]{3,2,1,0:T(2,128)(2,1)}), bf16[128,5,2,128]{3,2,1,0:T(2,128)(2,1)}, u32[]{:S(2)}, u32[]{:S(2)}) async-start(bf16[128,5,2,128]{3,2,1,0:T(2,128)(2,1)} %bitcast.27), calls=%async_computation.4 | async-start | bytes 655360 | tf_op jit(solution)/shard_map/all_to_all | solution.py:360
  130.3 21.6 %collective-permute-start.5 = (bf16[8,256,128]{2,1,0:T(8,128)(2,1)}, bf16[8,256,128]{2,1,0:T(8,128)(2,1)}, u32[]{:S(2)}, u32[]{:S(2)}) collective-permute-start(bf16[8,256,128]{2,1,0:T(8,128)(2,1)} %get-tuple-element.32.refs_1_.refs_4_), channel_id=1, source_target_pairs={{1,0},{2,1},{3,2},{4,3},{5,4},{6,5},{7,6},{8,7},{9,8},{10,9},{11,1... | collective-permute-start | bytes 1572872 | tf_op jit(solution)/shard_map/ppermute | solution.py:350
  137.3 20.2 %collective-permute-start.4 = (bf16[8,256,128]{2,1,0:T(8,128)(2,1)}, bf16[8,256,128]{2,1,0:T(8,128)(2,1)}, u32[]{:S(2)}, u32[]{:S(2)}) collective-permute-start(bf16[8,256,128]{2,1,0:T(8,128)(2,1)} %get-tuple-element.32.refs_1_.refs_4_), channel_id=1, source_target_pairs={{0,1},{1,2},{2,3},{3,4},{4,5},{5,6},{6,7},{7,8},{8,9},{9,10},{10,1... | collective-permute-start | bytes 1572872 | tf_op jit(solution)/shard_map/ppermute | solution.py:350
  143.8 22.5 %all-to-all-start.5 = ((bf16[128,5,2,128]{3,2,1,0:T(2,128)(2,1)}), bf16[128,5,2,128]{3,2,1,0:T(2,128)(2,1)}, u32[]{:S(2)}, u32[]{:S(2)}) async-start(bf16[128,5,2,128]{3,2,1,0:T(2,128)(2,1)} %bitcast.24), calls=%async_computation.5 | async-start | bytes 655360 | tf_op jit(solution)/shard_map/all_to_all | solution.py:360
  171.4 17.1 %all-to-all-start.6 = ((bf16[128,5,2,128]{3,2,1,0:T(2,128)(2,1)}), bf16[128,5,2,128]{3,2,1,0:T(2,128)(2,1)}, u32[]{:S(2)}, u32[]{:S(2)}) async-start(bf16[128,5,2,128]{3,2,1,0:T(2,128)(2,1)} %bitcast.28), calls=%async_computation.6 | async-start | bytes 655360 | tf_op jit(solution)/shard_map/all_to_all | solution.py:360
  177.4 21.6 %collective-permute-start.7 = (bf16[8,256,128]{2,1,0:T(8,128)(2,1)}, bf16[8,256,128]{2,1,0:T(8,128)(2,1)}, u32[]{:S(2)}, u32[]{:S(2)}) collective-permute-start(bf16[8,256,128]{2,1,0:T(8,128)(2,1)} %get-tuple-element.35.refs_1_), channel_id=1, source_target_pairs={{1,0},{2,1},{3,2},{4,3},{5,4},{6,5},{7,6},{8,7},{9,8},{10,9},{11,1... | collective-permute-start | bytes 1572872 | tf_op jit(solution)/shard_map/ppermute | solution.py:350
  184.3 20.2 %collective-permute-start.6 = (bf16[8,256,128]{2,1,0:T(8,128)(2,1)}, bf16[8,256,128]{2,1,0:T(8,128)(2,1)}, u32[]{:S(2)}, u32[]{:S(2)}) collective-permute-start(bf16[8,256,128]{2,1,0:T(8,128)(2,1)} %get-tuple-element.35.refs_1_), channel_id=1, source_target_pairs={{0,1},{1,2},{2,3},{3,4},{4,5},{5,6},{6,7},{7,8},{8,9},{9,10},{10,1... | collective-permute-start | bytes 1572872 | tf_op jit(solution)/shard_map/ppermute | solution.py:350
  190.9 22.4 %all-to-all-start.7 = ((bf16[128,5,2,128]{3,2,1,0:T(2,128)(2,1)}), bf16[128,5,2,128]{3,2,1,0:T(2,128)(2,1)}, u32[]{:S(2)}, u32[]{:S(2)}) async-start(bf16[128,5,2,128]{3,2,1,0:T(2,128)(2,1)} %bitcast.23), calls=%async_computation.7 | async-start | bytes 655360 | tf_op jit(solution)/shard_map/all_to_all | solution.py:360

commit v2 on v1

--- a/solution.py
+++ b/solution.py
@@ -381,10 +381,10 @@
     rows = band + band % 2
     first_group = (lax.axis_index(AXES) - 1) * groups
     places = (first_group.reshape(1), neighbours, near_mask)
-    packed = pack(spectra_past[:, 0], band, rows)
+    packed = pack(spectra_past[:, 0], band, band)
     opening = exchange(packed, messages)
     past = window(currents_past)
-    bands = [(opening, lag * rows, LAGS * rows) for lag in range(LAGS)]
+    bands = [(opening, lag * band, LAGS * band) for lag in range(LAGS)]
     windows = [(past, 0), (past, 1)]
     rays = pad_rays(ray_in, ray_out, child_shift, band, rows)
     weights = far_weights(far_sources, far_delays, translation)
@@ -397,7 +397,8 @@
         if rest:
             current, spectra = rest
             moved = exchange(spectra, messages)
-            nearby = window(current)
+            after = shifted(current, -1)
+            nearby = [shifted(current, 1), current, after]
             windows = [(nearby, None), windows[0]]
             bands = [(moved, 0, rows), bands[0]]
     return results

time: 219 us -> 218 us (level)
  no operation moved by 1% of the time
where the time goes in v2:
time: 218 us; the launch traced here: 217 us
  starting transfers between devices  95.7 us (44%)
  Pallas kernels  73.5 us (34%)
  waiting for transfers between devices  47.3 us (22%)
    all_to_all x8, starting transfers between devices, exchange(): moved = lax.all_to_all(cut, AXES, split_axis=0, concat_axis=0, tiled=True)  58.9 us
    ppermute x8, starting transfers between devices, shifted(): return lax.ppermute(block, AXES, route)  36.8 us
    pallas_call x4, Pallas kernels, near_field(): pl.pallas_call(functools.partial(near_kernel, step, leads), in_specs=[pl....  35.1 us
    all_to_all x8, waiting for transfers between devices, exchange(): moved = lax.all_to_all(cut, AXES, split_axis=0, concat_axis=0, tiled=True)  30.9 us
    pallas_call x4, Pallas kernels, solve(): pl.pallas_call(functools.partial(solve_kernel, step, aliased), in_specs=[...  19.7 us
    ppermute x8, waiting for transfers between devices, shifted(): return lax.ppermute(block, AXES, route)  16.4 us
    pallas_call x4, Pallas kernels, translate(): pl.pallas_call(functools.partial(translate_kernel, rows, tuple(places)),...  9.79 us
  transfers between devices with their start and end apart: 16, of which 8 were waited for; matrix products, arithmetic and copies ran while one was open for 0% of the time, Pallas kernels for 25%

profile of v2, /device:TPU:1, one launch (start us, length us, event | category | flops | bytes accessed | tf_op | source)
XLA Modules:
  0.0 217.0 jit_solution(14820941122856993499)
XLA Ops:
  0.0 8.2 %collective-permute-start.1 = (bf16[2,8,256,128]{3,2,1,0:T(8,128)(2,1)}, bf16[2,8,256,128]{3,2,1,0:T(8,128)(2,1)}, u32[]{:S(2)}, u32[]{:S(2)}) collective-permute-start(bf16[2,8,256,128]{3,2,1,0:T(8,128)(2,1)} %refs_4_.8), channel_id=1, source_target_pairs={{1,0},{2,1},{3,2},{4,3},{5,4},{6,5},{7,6},{8,7},{9,8},{10,9},{11,1... | collective-permute-start | bytes 3145736 | tf_op jit(solution)/shard_map/ppermute | solution.py:350
  12.2 10.4 %all-to-all-start = ((bf16[128,9,2,128]{3,2,1,0:T(2,128)(2,1)}), bf16[128,9,2,128]{3,2,1,0:T(2,128)(2,1)}, u32[]{:S(2)}, u32[]{:S(2)}) async-start(bf16[128,9,2,128]{3,2,1,0:T(2,128)(2,1)} %bitcast.21), calls=%async_computation | async-start | bytes 1179648 | tf_op jit(solution)/shard_map/all_to_all | solution.py:360
  29.6 22.2 %all-to-all-done = bf16[128,9,2,128]{3,2,1,0:T(2,128)(2,1)} async-done(((bf16[128,9,2,128]{3,2,1,0:T(2,128)(2,1)}), bf16[128,9,2,128]{3,2,1,0:T(2,128)(2,1)}, u32[]{:S(2)}, u32[]{:S(2)}) %all-to-all-start) | async-done | bytes 589856 | tf_op jit(solution)/shard_map/all_to_all | solution.py:360
  54.1 4.6 %all-to-all-start.1 = ((bf16[128,5,2,128]{3,2,1,0:T(2,128)(2,1)}), bf16[128,5,2,128]{3,2,1,0:T(2,128)(2,1)}, u32[]{:S(2)}, u32[]{:S(2)}) async-start(bf16[128,5,2,128]{3,2,1,0:T(2,128)(2,1)} %bitcast.23), calls=%async_computation.1 | async-start | bytes 655360 | tf_op jit(solution)/shard_map/all_to_all | solution.py:360
  58.8 8.8 %near.4.refs_3_ = f32[8,256,128]{2,1,0:T(8,128)} custom-call(s32[1]{0:T(128)} %bitcast.8.first_ref, s32[8,6]{1,0:T(8,128)} %ids_ref.7, s32[8,6]{1,0:T(8,128)} %mask_ref.7, f32[4,8,256,128]{3,2,1,0:T(8,128)} %incident_ref.7, bf16[8,6,2,256,256]{4,3,2,1,0:T(8,128)(2,1)} %blocks_ref.7, bf16[2,8,256,128]{3,2,1,0:T(8,128)(2,1)} %collective-permute-done.refs_0_.refs_3_, ...), custom_call_target="tpu_custom_call" | custom-call | tf_op jit(solution)/shard_map/near/pallas_call | solution.py:241
  69.6 5.1 %solve.4 = (bf16[4,8,256,128]{3,2,1,0:T(8,128)(2,1)}, bf16[8,256,128]{2,1,0:T(8,128)(2,1)}, bf16[1280,128]{1,0:T(8,128)(2,1)}) custom-call(bf16[1280,128]{1,0:T(8,128)(2,1)} %bitcast.7.refs_0_, bf16[256,1280]{1,0:T(8,128)(2,1)} %get-tuple-element.25.refs_1_, bf16[1280,128]{1,0:T(8,128)(2,1)} %get-tuple-element.26.refs_2_, f32[8,256,128]{2,1,0:T(8,128)} %near.4.refs_3_, ...), custom_call_target="tpu_custom_call" | custom-call | tf_op jit(solution)/shard_map/solve/pallas_call | solution.py:329
  74.7 7.9 %all-to-all-start.2 = ((bf16[128,5,2,128]{3,2,1,0:T(2,128)(2,1)}), bf16[128,5,2,128]{3,2,1,0:T(2,128)(2,1)}, u32[]{:S(2)}, u32[]{:S(2)}) async-start(bf16[128,5,2,128]{3,2,1,0:T(2,128)(2,1)} %bitcast.29), calls=%async_computation.2 | async-start | bytes 655360 | tf_op jit(solution)/shard_map/all_to_all | solution.py:360
  82.6 7.0 %collective-permute-start.3 = (bf16[8,256,128]{2,1,0:T(8,128)(2,1)}, bf16[8,256,128]{2,1,0:T(8,128)(2,1)}, u32[]{:S(2)}, u32[]{:S(2)}) collective-permute-start(bf16[8,256,128]{2,1,0:T(8,128)(2,1)} %get-tuple-element.29.refs_1_.refs_4_), channel_id=1, source_target_pairs={{1,0},{2,1},{3,2},{4,3},{5,4},{6,5},{7,6},{8,7},{9,8},{10,9},{11,1... | collective-permute-start | bytes 1572872 | tf_op jit(solution)/shard_map/ppermute | solution.py:350
  96.3 8.1 %all-to-all-start.3 = ((bf16[128,5,2,128]{3,2,1,0:T(2,128)(2,1)}), bf16[128,5,2,128]{3,2,1,0:T(2,128)(2,1)}, u32[]{:S(2)}, u32[]{:S(2)}) async-start(bf16[128,5,2,128]{3,2,1,0:T(2,128)(2,1)} %bitcast.22), calls=%async_computation.3 | async-start | bytes 655360 | tf_op jit(solution)/shard_map/all_to_all | solution.py:360
  104.4 5.3 %collective-permute-done.2.refs_0_.refs_3_ = bf16[8,256,128]{2,1,0:T(8,128)(2,1)} collective-permute-done((bf16[8,256,128]{2,1,0:T(8,128)(2,1)}, bf16[8,256,128]{2,1,0:T(8,128)(2,1)}, u32[]{:S(2)}, u32[]{:S(2)}) %collective-permute-start.2) | collective-permute-done | bytes 524320 | tf_op jit(solution)/shard_map/ppermute | solution.py:350
  109.7 8.8 %near.5.refs_3_ = f32[8,256,128]{2,1,0:T(8,128)} custom-call(s32[1]{0:T(128)} %bitcast.8.first_ref, s32[8,6]{1,0:T(8,128)} %ids_ref.7, s32[8,6]{1,0:T(8,128)} %mask_ref.7, f32[4,8,256,128]{3,2,1,0:T(8,128)} %incident_ref.7, bf16[8,6,2,256,256]{4,3,2,1,0:T(8,128)(2,1)} %blocks_ref.7, bf16[8,256,128]{2,1,0:T(8,128)(2,1)} %collective-permute-done.2.refs_0_.refs_3_, ...), custom_call_target="tpu_custom_call" | custom-call | tf_op jit(solution)/shard_map/near/pallas_call | solution.py:241
  118.5 5.1 %solve.5 = (bf16[4,8,256,128]{3,2,1,0:T(8,128)(2,1)}, bf16[8,256,128]{2,1,0:T(8,128)(2,1)}, bf16[1280,128]{1,0:T(8,128)(2,1)}) custom-call(bf16[1280,128]{1,0:T(8,128)(2,1)} %bitcast.12.refs_0_, bf16[256,1280]{1,0:T(8,128)(2,1)} %get-tuple-element.25.refs_1_, bf16[1280,128]{1,0:T(8,128)(2,1)} %get-tuple-element.26.refs_2_, ...), custom_call_target="tpu_custom_call", output_to_operand_aliasing={{0}: (6, {})} | custom-call | tf_op jit(solution)/shard_map/solve/pallas_call | solution.py:329
  123.7 5.9 %all-to-all-start.4 = ((bf16[128,5,2,128]{3,2,1,0:T(2,128)(2,1)}), bf16[128,5,2,128]{3,2,1,0:T(2,128)(2,1)}, u32[]{:S(2)}, u32[]{:S(2)}) async-start(bf16[128,5,2,128]{3,2,1,0:T(2,128)(2,1)} %bitcast.27), calls=%async_computation.4 | async-start | bytes 655360 | tf_op jit(solution)/shard_map/all_to_all | solution.py:360
  129.6 7.0 %collective-permute-start.5 = (bf16[8,256,128]{2,1,0:T(8,128)(2,1)}, bf16[8,256,128]{2,1,0:T(8,128)(2,1)}, u32[]{:S(2)}, u32[]{:S(2)}) collective-permute-start(bf16[8,256,128]{2,1,0:T(8,128)(2,1)} %get-tuple-element.32.refs_1_.refs_4_), channel_id=1, source_target_pairs={{1,0},{2,1},{3,2},{4,3},{5,4},{6,5},{7,6},{8,7},{9,8},{10,9},{11,1... | collective-permute-start | bytes 1572872 | tf_op jit(solution)/shard_map/ppermute | solution.py:350
  143.1 8.1 %all-to-all-start.5 = ((bf16[128,5,2,128]{3,2,1,0:T(2,128)(2,1)}), bf16[128,5,2,128]{3,2,1,0:T(2,128)(2,1)}, u32[]{:S(2)}, u32[]{:S(2)}) async-start(bf16[128,5,2,128]{3,2,1,0:T(2,128)(2,1)} %bitcast.25), calls=%async_computation.5 | async-start | bytes 655360 | tf_op jit(solution)/shard_map/all_to_all | solution.py:360
  151.2 5.6 %collective-permute-done.4.refs_0_.refs_3_ = bf16[8,256,128]{2,1,0:T(8,128)(2,1)} collective-permute-done((bf16[8,256,128]{2,1,0:T(8,128)(2,1)}, bf16[8,256,128]{2,1,0:T(8,128)(2,1)}, u32[]{:S(2)}, u32[]{:S(2)}) %collective-permute-start.4) | collective-permute-done | bytes 524320 | tf_op jit(solution)/shard_map/ppermute | solution.py:350
  156.7 8.8 %near.6.refs_3_ = f32[8,256,128]{2,1,0:T(8,128)} custom-call(s32[1]{0:T(128)} %bitcast.8.first_ref, s32[8,6]{1,0:T(8,128)} %ids_ref.7, s32[8,6]{1,0:T(8,128)} %mask_ref.7, f32[4,8,256,128]{3,2,1,0:T(8,128)} %incident_ref.7, bf16[8,6,2,256,256]{4,3,2,1,0:T(8,128)(2,1)} %blocks_ref.7, bf16[8,256,128]{2,1,0:T(8,128)(2,1)} %collective-permute-done.4.refs_0_.refs_3_, ...), custom_call_target="tpu_custom_call" | custom-call | tf_op jit(solution)/shard_map/near/pallas_call | solution.py:241
  165.5 5.1 %solve.6 = (bf16[4,8,256,128]{3,2,1,0:T(8,128)(2,1)}, bf16[8,256,128]{2,1,0:T(8,128)(2,1)}, bf16[1280,128]{1,0:T(8,128)(2,1)}) custom-call(bf16[1280,128]{1,0:T(8,128)(2,1)} %bitcast.16.refs_0_, bf16[256,1280]{1,0:T(8,128)(2,1)} %get-tuple-element.25.refs_1_, bf16[1280,128]{1,0:T(8,128)(2,1)} %get-tuple-element.26.refs_2_, ...), custom_call_target="tpu_custom_call", output_to_operand_aliasing={{0}: (6, {})} | custom-call | tf_op jit(solution)/shard_map/solve/pallas_call | solution.py:329
  170.7 5.9 %all-to-all-start.6 = ((bf16[128,5,2,128]{3,2,1,0:T(2,128)(2,1)}), bf16[128,5,2,128]{3,2,1,0:T(2,128)(2,1)}, u32[]{:S(2)}, u32[]{:S(2)}) async-start(bf16[128,5,2,128]{3,2,1,0:T(2,128)(2,1)} %bitcast.28), calls=%async_computation.6 | async-start | bytes 655360 | tf_op jit(solution)/shard_map/all_to_all | solution.py:360
  176.6 7.0 %collective-permute-start.7 = (bf16[8,256,128]{2,1,0:T(8,128)(2,1)}, bf16[8,256,128]{2,1,0:T(8,128)(2,1)}, u32[]{:S(2)}, u32[]{:S(2)}) collective-permute-start(bf16[8,256,128]{2,1,0:T(8,128)(2,1)} %get-tuple-element.35.refs_1_), channel_id=1, source_target_pairs={{1,0},{2,1},{3,2},{4,3},{5,4},{6,5},{7,6},{8,7},{9,8},{10,9},{11,1... | collective-permute-start | bytes 1572872 | tf_op jit(solution)/shard_map/ppermute | solution.py:350
  190.1 8.1 %all-to-all-start.7 = ((bf16[128,5,2,128]{3,2,1,0:T(2,128)(2,1)}), bf16[128,5,2,128]{3,2,1,0:T(2,128)(2,1)}, u32[]{:S(2)}, u32[]{:S(2)}) async-start(bf16[128,5,2,128]{3,2,1,0:T(2,128)(2,1)} %bitcast.24), calls=%async_computation.7 | async-start | bytes 655360 | tf_op jit(solution)/shard_map/all_to_all | solution.py:360
  198.2 5.5 %collective-permute-done.6.refs_0_ = bf16[8,256,128]{2,1,0:T(8,128)(2,1)} collective-permute-done((bf16[8,256,128]{2,1,0:T(8,128)(2,1)}, bf16[8,256,128]{2,1,0:T(8,128)(2,1)}, u32[]{:S(2)}, u32[]{:S(2)}) %collective-permute-start.6) | collective-permute-done | bytes 524320 | tf_op jit(solution)/shard_map/ppermute | solution.py:350
  203.8 8.8 %near.7.refs_3_ = f32[8,256,128]{2,1,0:T(8,128)} custom-call(s32[1]{0:T(128)} %bitcast.8.first_ref, s32[8,6]{1,0:T(8,128)} %ids_ref.7, s32[8,6]{1,0:T(8,128)} %mask_ref.7, f32[4,8,256,128]{3,2,1,0:T(8,128)} %incident_ref.7, bf16[8,6,2,256,256]{4,3,2,1,0:T(8,128)(2,1)} %blocks_ref.7, bf16[8,256,128]{2,1,0:T(8,128)(2,1)} %collective-permute-done.6.refs_0_, ...), custom_call_target="tpu_custom_call" | custom-call | tf_op jit(solution)/shard_map/near/pallas_call | solution.py:241
  212.6 4.3 %solve.7 = bf16[4,8,256,128]{3,2,1,0:T(8,128)(2,1)} custom-call(bf16[1280,128]{1,0:T(8,128)(2,1)} %bitcast.20.refs_0_, bf16[256,1280]{1,0:T(8,128)(2,1)} %get-tuple-element.25.refs_1_, bf16[1280,128]{1,0:T(8,128)(2,1)} %get-tuple-element.26.refs_2_, f32[8,256,128]{2,1,0:T(8,128)} %near.7.refs_3_, ...), custom_call_target="tpu_custom_call", output_to_operand_aliasing={{}: (6, {})} | custom-call | tf_op jit(solution)/shard_map/solve/pallas_call | solution.py:329
  (23 shorter events, 35.2 us)
Async XLA Ops:
  0.0 58.8 %collective-permute-start.1 = (bf16[2,8,256,128]{3,2,1,0:T(8,128)(2,1)}, bf16[2,8,256,128]{3,2,1,0:T(8,128)(2,1)}, u32[]{:S(2)}, u32[]{:S(2)}) collective-permute-start(bf16[2,8,256,128]{3,2,1,0:T(8,128)(2,1)} %refs_4_.8), channel_id=1, source_target_pairs={{1,0},{2,1},{3,2},{4,3},{5,4},{6,5},{7,6},{8,7},{9,8},{10,9},{11,1... | collective-permute-start | bytes 3145736 | tf_op jit(solution)/shard_map/ppermute | solution.py:350
  8.2 50.6 %collective-permute-start = (bf16[2,8,256,128]{3,2,1,0:T(8,128)(2,1)}, bf16[2,8,256,128]{3,2,1,0:T(8,128)(2,1)}, u32[]{:S(2)}, u32[]{:S(2)}) collective-permute-start(bf16[2,8,256,128]{3,2,1,0:T(8,128)(2,1)} %refs_4_.8), channel_id=1, source_target_pairs={{0,1},{1,2},{2,3},{3,4},{4,5},{5,6},{6,7},{7,8},{8,9},{9,10},{10,1... | collective-permute-start | bytes 3145736 | tf_op jit(solution)/shard_map/ppermute | solution.py:350
  12.2 39.6 %all-to-all-start = ((bf16[128,9,2,128]{3,2,1,0:T(2,128)(2,1)}), bf16[128,9,2,128]{3,2,1,0:T(2,128)(2,1)}, u32[]{:S(2)}, u32[]{:S(2)}) async-start(bf16[128,9,2,128]{3,2,1,0:T(2,128)(2,1)} %bitcast.21), calls=%async_computation | async-start | bytes 1179648 | tf_op jit(solution)/shard_map/all_to_all | solution.py:360
  54.1 15.4 %all-to-all-start.1 = ((bf16[128,5,2,128]{3,2,1,0:T(2,128)(2,1)}), bf16[128,5,2,128]{3,2,1,0:T(2,128)(2,1)}, u32[]{:S(2)}, u32[]{:S(2)}) async-start(bf16[128,5,2,128]{3,2,1,0:T(2,128)(2,1)} %bitcast.23), calls=%async_computation.1 | async-start | bytes 655360 | tf_op jit(solution)/shard_map/all_to_all | solution.py:360
  74.7 19.0 %all-to-all-start.2 = ((bf16[128,5,2,128]{3,2,1,0:T(2,128)(2,1)}), bf16[128,5,2,128]{3,2,1,0:T(2,128)(2,1)}, u32[]{:S(2)}, u32[]{:S(2)}) async-start(bf16[128,5,2,128]{3,2,1,0:T(2,128)(2,1)} %bitcast.29), calls=%async_computation.2 | async-start | bytes 655360 | tf_op jit(solution)/shard_map/all_to_all | solution.py:360
  82.6 21.8 %collective-permute-start.3 = (bf16[8,256,128]{2,1,0:T(8,128)(2,1)}, bf16[8,256,128]{2,1,0:T(8,128)(2,1)}, u32[]{:S(2)}, u32[]{:S(2)}) collective-permute-start(bf16[8,256,128]{2,1,0:T(8,128)(2,1)} %get-tuple-element.29.refs_1_.refs_4_), channel_id=1, source_target_pairs={{1,0},{2,1},{3,2},{4,3},{5,4},{6,5},{7,6},{8,7},{9,8},{10,9},{11,1... | collective-permute-start | bytes 1572872 | tf_op jit(solution)/shard_map/ppermute | solution.py:350
  89.6 20.2 %collective-permute-start.2 = (bf16[8,256,128]{2,1,0:T(8,128)(2,1)}, bf16[8,256,128]{2,1,0:T(8,128)(2,1)}, u32[]{:S(2)}, u32[]{:S(2)}) collective-permute-start(bf16[8,256,128]{2,1,0:T(8,128)(2,1)} %get-tuple-element.29.refs_1_.refs_4_), channel_id=1, source_target_pairs={{0,1},{1,2},{2,3},{3,4},{4,5},{5,6},{6,7},{7,8},{8,9},{9,10},{10,1... | collective-permute-start | bytes 1572872 | tf_op jit(solution)/shard_map/ppermute | solution.py:350
  96.3 22.2 %all-to-all-start.3 = ((bf16[128,5,2,128]{3,2,1,0:T(2,128)(2,1)}), bf16[128,5,2,128]{3,2,1,0:T(2,128)(2,1)}, u32[]{:S(2)}, u32[]{:S(2)}) async-start(bf16[128,5,2,128]{3,2,1,0:T(2,128)(2,1)} %bitcast.22), calls=%async_computation.3 | async-start | bytes 655360 | tf_op jit(solution)/shard_map/all_to_all | solution.py:360
  123.7 17.0 %all-to-all-start.4 = ((bf16[128,5,2,128]{3,2,1,0:T(2,128)(2,1)}), bf16[128,5,2,128]{3,2,1,0:T(2,128)(2,1)}, u32[]{:S(2)}, u32[]{:S(2)}) async-start(bf16[128,5,2,128]{3,2,1,0:T(2,128)(2,1)} %bitcast.27), calls=%async_computation.4 | async-start | bytes 655360 | tf_op jit(solution)/shard_map/all_to_all | solution.py:360
  129.6 21.6 %collective-permute-start.5 = (bf16[8,256,128]{2,1,0:T(8,128)(2,1)}, bf16[8,256,128]{2,1,0:T(8,128)(2,1)}, u32[]{:S(2)}, u32[]{:S(2)}) collective-permute-start(bf16[8,256,128]{2,1,0:T(8,128)(2,1)} %get-tuple-element.32.refs_1_.refs_4_), channel_id=1, source_target_pairs={{1,0},{2,1},{3,2},{4,3},{5,4},{6,5},{7,6},{8,7},{9,8},{10,9},{11,1... | collective-permute-start | bytes 1572872 | tf_op jit(solution)/shard_map/ppermute | solution.py:350
  136.5 20.2 %collective-permute-start.4 = (bf16[8,256,128]{2,1,0:T(8,128)(2,1)}, bf16[8,256,128]{2,1,0:T(8,128)(2,1)}, u32[]{:S(2)}, u32[]{:S(2)}) collective-permute-start(bf16[8,256,128]{2,1,0:T(8,128)(2,1)} %get-tuple-element.32.refs_1_.refs_4_), channel_id=1, source_target_pairs={{0,1},{1,2},{2,3},{3,4},{4,5},{5,6},{6,7},{7,8},{8,9},{9,10},{10,1... | collective-permute-start | bytes 1572872 | tf_op jit(solution)/shard_map/ppermute | solution.py:350
  143.1 22.5 %all-to-all-start.5 = ((bf16[128,5,2,128]{3,2,1,0:T(2,128)(2,1)}), bf16[128,5,2,128]{3,2,1,0:T(2,128)(2,1)}, u32[]{:S(2)}, u32[]{:S(2)}) async-start(bf16[128,5,2,128]{3,2,1,0:T(2,128)(2,1)} %bitcast.25), calls=%async_computation.5 | async-start | bytes 655360 | tf_op jit(solution)/shard_map/all_to_all | solution.py:360
  170.7 17.1 %all-to-all-start.6 = ((bf16[128,5,2,128]{3,2,1,0:T(2,128)(2,1)}), bf16[128,5,2,128]{3,2,1,0:T(2,128)(2,1)}, u32[]{:S(2)}, u32[]{:S(2)}) async-start(bf16[128,5,2,128]{3,2,1,0:T(2,128)(2,1)} %bitcast.28), calls=%async_computation.6 | async-start | bytes 655360 | tf_op jit(solution)/shard_map/all_to_all | solution.py:360
  176.6 21.6 %collective-permute-start.7 = (bf16[8,256,128]{2,1,0:T(8,128)(2,1)}, bf16[8,256,128]{2,1,0:T(8,128)(2,1)}, u32[]{:S(2)}, u32[]{:S(2)}) collective-permute-start(bf16[8,256,128]{2,1,0:T(8,128)(2,1)} %get-tuple-element.35.refs_1_), channel_id=1, source_target_pairs={{1,0},{2,1},{3,2},{4,3},{5,4},{6,5},{7,6},{8,7},{9,8},{10,9},{11,1... | collective-permute-start | bytes 1572872 | tf_op jit(solution)/shard_map/ppermute | solution.py:350
  183.6 20.2 %collective-permute-start.6 = (bf16[8,256,128]{2,1,0:T(8,128)(2,1)}, bf16[8,256,128]{2,1,0:T(8,128)(2,1)}, u32[]{:S(2)}, u32[]{:S(2)}) collective-permute-start(bf16[8,256,128]{2,1,0:T(8,128)(2,1)} %get-tuple-element.35.refs_1_), channel_id=1, source_target_pairs={{0,1},{1,2},{2,3},{3,4},{4,5},{5,6},{6,7},{7,8},{8,9},{9,10},{10,1... | collective-permute-start | bytes 1572872 | tf_op jit(solution)/shard_map/ppermute | solution.py:350
  190.1 22.4 %all-to-all-start.7 = ((bf16[128,5,2,128]{3,2,1,0:T(2,128)(2,1)}), bf16[128,5,2,128]{3,2,1,0:T(2,128)(2,1)}, u32[]{:S(2)}, u32[]{:S(2)}) async-start(bf16[128,5,2,128]{3,2,1,0:T(2,128)(2,1)} %bitcast.24), calls=%async_computation.7 | async-start | bytes 655360 | tf_op jit(solution)/shard_map/all_to_all | solution.py:360
